TPU v7x, 32 devices: a whole 2x2x4 slice. The times are simulated.
32 devices in a mesh: pair: 8 (over z, x), row: 4 (over y, core).
Axes of the slice: x: 2, y: 2, z: 4, core: 2. Of those that a mesh axis runs over, the one named last changes fastest.
Arguments:
- records: bfloat16 [128, 4096, 8], P('row', 'pair'), may hold values from -10 to 10
- offsets: float32 [8, 128], P('pair', 'row'), may hold values from -1 to 1
- counts: int32 [8], replicated, may hold values from 64 to 128, as said below
- damping: float32 [1], replicated, may hold values from 0.1 to 1
Outputs:
- offset_step: float32 [8, 128], P('pair', 'row')
Inputs may be any that keep to these rules, and one draw needn't show every extreme that they name: Channel i of block b is live when i < counts[b]; in every draw some block has all 128 channels live.
All inputs are finite; a program needn't handle non-finite values.
Results may differ from a plain program's by a relative error of at most 0.0044.
Values may be sent and summed in bfloat16 or wider, within the bound.
No kernel may reach another device: no remote copies, remote signals or barrier semaphores. Data moves between devices by JAX's collectives and lax.ppermute only.
A program may use at most 64 MiB of HBM per device.

v0:
```python
import math
import jax
import jax.numpy as jnp
from jax import lax
from jax.sharding import PartitionSpec as P

CB = 128
NF = 512
NLAG = 256


def band_table(row_start, row_count, samples, first_bin, freq_count):
    sample_ids = row_start + jnp.arange(row_count, dtype=jnp.int32)
    freq_bins = first_bin + jnp.arange(freq_count, dtype=jnp.int32)
    phase_ids = sample_ids[:, None] * freq_bins[None, :] % samples
    angles = phase_ids.astype(jnp.float32) * (2.0 * math.pi / samples)
    return jnp.concatenate([jnp.cos(angles), jnp.sin(angles)], axis=1)


def lag_weights(samples, first_bin, freq_count, lag_count):
    freq_bins = first_bin + jnp.arange(freq_count, dtype=jnp.int32)
    lag_ids = 1 + jnp.arange(lag_count, dtype=jnp.int32)
    phase_ids = freq_bins[:, None] * lag_ids[None, :] % samples
    angles = phase_ids.astype(jnp.float32) * (2.0 * math.pi / samples)
    centre = (jnp.arange(freq_count, dtype=jnp.float32) + 0.5) * (math.pi / freq_count)
    weight = jnp.sin(centre) ** 2
    return (-2.0 * weight[:, None] * jnp.sin(angles)).astype(jnp.bfloat16)


def pair_stats(own_spec, partners, lag_table, angular):
    own_re = own_spec[:, 0].astype(jnp.float32)
    own_im = own_spec[:, 1].astype(jnp.float32)
    far_re = partners[:, :, 0].astype(jnp.float32)
    far_im = partners[:, :, 1].astype(jnp.float32)
    cross_re = own_re * far_re + own_im * far_im
    cross_im = own_im * far_re - own_re * far_im
    stacked = jnp.stack([cross_im, angular * cross_re]).astype(jnp.bfloat16)
    lagged = jnp.dot(stacked, lag_table, preferred_element_type=jnp.float32)
    residual = lagged[0]
    jacobian = lagged[1]
    return (jnp.sum(jacobian * jacobian, axis=-1), jnp.sum(jacobian * residual, axis=-1))


def per_device(records, offsets, counts, damping):
    nblock = lax.axis_size("pair")
    block_rank = lax.axis_index("pair")
    quarter = lax.axis_index("row")
    relaid = lax.all_to_all(records, "pair", split_axis=2, concat_axis=1, tiled=True)
    signal = relaid[:, :, 0]
    channels = signal.shape[0]
    samples = signal.shape[1]
    first_bin = samples // 8
    block_len = samples // 8

    def accumulate(partial_value, turn_index):
        first_row = turn_index * block_len
        segment = lax.dynamic_slice_in_dim(signal, first_row, block_len, 1)
        dft_table = band_table(first_row, block_len, samples, first_bin, NF)
        table_high = dft_table.astype(jnp.bfloat16)
        table_low = (dft_table - table_high.astype(jnp.float32)).astype(jnp.bfloat16)
        partial_value = partial_value + jnp.dot(
            segment, table_high, preferred_element_type=jnp.float32
        )
        partial_value = partial_value + jnp.dot(
            segment, table_low, preferred_element_type=jnp.float32
        )
        return (partial_value, None)

    spectrum, _ = lax.scan(
        accumulate, jnp.zeros((channels, 2 * NF), jnp.float32), jnp.arange(8, dtype=jnp.int32)
    )
    cosine_part = spectrum[:, :NF]
    sine_part = spectrum[:, NF:]
    angular = (first_bin + jnp.arange(NF, dtype=jnp.int32)).astype(jnp.float32) * (
        2.0 * math.pi / samples
    )
    shift_angle = offsets[0][:, None] * angular[None, :]
    shift_cos = jnp.cos(shift_angle)
    shift_sin = jnp.sin(shift_angle)
    real_part = cosine_part * shift_cos + sine_part * shift_sin
    imag_part = cosine_part * shift_sin - sine_part * shift_cos
    live_count = lax.dynamic_index_in_dim(counts, block_rank, keepdims=False)
    channel_ids = quarter * channels + jnp.arange(channels, dtype=jnp.int32)
    alive = (channel_ids < live_count).astype(jnp.float32)
    energy = jnp.mean(real_part * real_part + imag_part * imag_part, axis=1)
    weight_scale = alive / jnp.sqrt(energy + 1e-06)
    own_spec = jnp.stack(
        [real_part * weight_scale[:, None], imag_part * weight_scale[:, None]], axis=1
    ).astype(jnp.bfloat16)
    lag_table = lag_weights(samples, first_bin, NF, NLAG)
    segment = lax.all_gather(own_spec[None], "pair", axis=0, tiled=True)
    squares_part, products_part = pair_stats(own_spec, segment, lag_table, angular)
    partner_ids = jnp.arange(segment.shape[0], dtype=jnp.int32)
    keep_mask = (partner_ids > block_rank).astype(jnp.float32)[:, None]
    new_squares = squares_part * keep_mask
    new_products = products_part * keep_mask
    eye_blocks = jnp.eye(nblock, dtype=jnp.float32)
    onehot = (jnp.arange(nblock, dtype=jnp.int32) == block_rank).astype(jnp.float32)
    sq_t = new_squares.T
    pr_t = new_products.T
    crossing = sq_t[:, None, :] * onehot[None, :, None]
    diag_vals = sq_t + onehot[None, :] * jnp.sum(sq_t, axis=1, keepdims=True)
    hessian = diag_vals[:, :, None] * eye_blocks[None] - crossing - jnp.swapaxes(crossing, 1, 2)
    gradient = onehot[None, :] * jnp.sum(pr_t, axis=1, keepdims=True) - pr_t
    hessian, gradient = lax.psum((hessian, gradient), "pair")
    diagonal = jnp.diagonal(hessian, axis1=1, axis2=2)
    trace_sum = lax.psum(jnp.sum(diagonal), "row")
    level_mean = trace_sum / (nblock * CB)
    damped = damping[0] * (diagonal + level_mean)
    system = hessian + damped[:, :, None] * eye_blocks[None]
    factor = jnp.linalg.cholesky(system)
    update = -jax.scipy.linalg.cho_solve((factor, True), gradient[:, :, None])[:, :, 0]
    return lax.dynamic_slice_in_dim(update, block_rank, 1, 1).T


def solution(mesh):
    return jax.shard_map(
        per_device,
        mesh=mesh,
        in_specs=(P("row", "pair", None), P("pair", "row"), P(), P()),
        out_specs=P("pair", "row"),
        check_vma=False,
    )
```

profile of v0, /device:TPU:0, one launch (start us, length us, event | category | flops | bytes accessed | tf_op | source)
XLA Modules:
  0.0 172.0 jit_solution(3710374380044799579)
XLA Ops:
  0.0 0.0 copy-start.1
  0.0 1.7 %copy.35 = bf16[32,512,8]{1,0,2:T(8,128)(2,1)} copy(bf16[32,512,8]{1,2,0:T(8,128)(2,1)} %param.6) | data formatting | bytes 524288 | tf_op args[0]
  1.7 7.3 %all-to-all-start = ((bf16[32,512,8]{1,0,2:T(8,128)(2,1)}), bf16[32,512,8]{1,0,2:T(8,128)(2,1)S(1)}, u32[]{:S(2)}, u32[]{:S(2)}) async-start(bf16[32,512,8]{1,0,2:T(8,128)(2,1)} %copy.35), calls=%async_computation | async-start | bytes 524288 | tf_op jit(solution)/shard_map/all_to_all | solution.py:48
  9.1 0.1 copy.38
  9.2 0.0 copy-done.1
  9.2 0.6 dynamic_slice.20
  9.9 8.1 %all-to-all-done = bf16[32,512,8]{1,0,2:T(8,128)(2,1)S(1)} async-done(((bf16[32,512,8]{1,0,2:T(8,128)(2,1)}), bf16[32,512,8]{1,0,2:T(8,128)(2,1)S(1)}, u32[]{:S(2)}, u32[]{:S(2)}) %all-to-all-start) | async-done | bytes 262176 | tf_op jit(solution)/shard_map/all_to_all | solution.py:48
  18.0 0.0 copy-start
  18.0 48.9 %while.13 = (s32[]{:T(128)}, f32[32,1024]{1,0:T(8,128)S(1)}, s32[8]{0:T(128)S(1)}, bf16[32,4096]{1,0:T(8,128)(2,1)S(1)}, s32[]{:T(128)}, /*index=5*/s32[1]{0:T(128)}, s32[]{:T(128)}, s32[]{:T(128)}) while((s32[]{:T(128)}, f32[32,1024]{1,0:T(8,128)S(1)}, s32[8]{0:T(128)S(1)}, bf16[32,4096]{1,0:T(8,128)(2,1)S(1)}, s32[]{:T(128)}, ...), condition=%wide.region_1.2_spmd.clone, body=%wide.region_0.1_spmd.clone.sunk | while | flops 75596808 | bytes 6889645 | solution.py:69
  18.0 0.7 dynamic_slice.34
  19.4 4.1 %fusion.70 = (f32[512,512]{1,0:T(8,128)S(1)}, f32[512,512]{1,0:T(8,128)S(1)}) fusion(s32[512]{0:T(512)S(1)} %get-tuple-element.138, s32[512]{0:T(512)S(1)} %get-tuple-element.139), kind=kLoop, calls=%fused_computation.16.clone.1 | loop fusion | flops 3670016 | bytes 2101248 | tf_op jit(solution)/shard_map/while/body/eval_jaxpr/cos | solution.py:17
  23.5 0.3 fusion.71
  23.8 0.3 convolution_add_fusion.2
  24.1 0.7 dynamic_slice.34
  25.5 4.1 %fusion.70 = (f32[512,512]{1,0:T(8,128)S(1)}, f32[512,512]{1,0:T(8,128)S(1)}) fusion(s32[512]{0:T(512)S(1)} %get-tuple-element.138, s32[512]{0:T(512)S(1)} %get-tuple-element.139), kind=kLoop, calls=%fused_computation.16.clone.1 | loop fusion | flops 3670016 | bytes 2101248 | tf_op jit(solution)/shard_map/while/body/eval_jaxpr/cos | solution.py:17
  29.6 0.3 fusion.71
  29.9 0.3 convolution_add_fusion.2
  30.2 0.7 dynamic_slice.34
  31.6 4.1 %fusion.70 = (f32[512,512]{1,0:T(8,128)S(1)}, f32[512,512]{1,0:T(8,128)S(1)}) fusion(s32[512]{0:T(512)S(1)} %get-tuple-element.138, s32[512]{0:T(512)S(1)} %get-tuple-element.139), kind=kLoop, calls=%fused_computation.16.clone.1 | loop fusion | flops 3670016 | bytes 2101248 | tf_op jit(solution)/shard_map/while/body/eval_jaxpr/cos | solution.py:17
  35.8 0.3 fusion.71
  36.1 0.3 convolution_add_fusion.2
  36.3 0.7 dynamic_slice.34
  37.7 4.1 %fusion.70 = (f32[512,512]{1,0:T(8,128)S(1)}, f32[512,512]{1,0:T(8,128)S(1)}) fusion(s32[512]{0:T(512)S(1)} %get-tuple-element.138, s32[512]{0:T(512)S(1)} %get-tuple-element.139), kind=kLoop, calls=%fused_computation.16.clone.1 | loop fusion | flops 3670016 | bytes 2101248 | tf_op jit(solution)/shard_map/while/body/eval_jaxpr/cos | solution.py:17
  41.9 0.3 fusion.71
  42.2 0.3 convolution_add_fusion.2
  42.5 0.7 dynamic_slice.34
  43.8 4.1 %fusion.70 = (f32[512,512]{1,0:T(8,128)S(1)}, f32[512,512]{1,0:T(8,128)S(1)}) fusion(s32[512]{0:T(512)S(1)} %get-tuple-element.138, s32[512]{0:T(512)S(1)} %get-tuple-element.139), kind=kLoop, calls=%fused_computation.16.clone.1 | loop fusion | flops 3670016 | bytes 2101248 | tf_op jit(solution)/shard_map/while/body/eval_jaxpr/cos | solution.py:17
  48.0 0.3 fusion.71
  48.3 0.3 convolution_add_fusion.2
  48.6 0.7 dynamic_slice.34
  50.0 4.1 %fusion.70 = (f32[512,512]{1,0:T(8,128)S(1)}, f32[512,512]{1,0:T(8,128)S(1)}) fusion(s32[512]{0:T(512)S(1)} %get-tuple-element.138, s32[512]{0:T(512)S(1)} %get-tuple-element.139), kind=kLoop, calls=%fused_computation.16.clone.1 | loop fusion | flops 3670016 | bytes 2101248 | tf_op jit(solution)/shard_map/while/body/eval_jaxpr/cos | solution.py:17
  54.1 0.3 fusion.71
  54.4 0.3 convolution_add_fusion.2
  54.7 0.7 dynamic_slice.34
  56.1 4.1 %fusion.70 = (f32[512,512]{1,0:T(8,128)S(1)}, f32[512,512]{1,0:T(8,128)S(1)}) fusion(s32[512]{0:T(512)S(1)} %get-tuple-element.138, s32[512]{0:T(512)S(1)} %get-tuple-element.139), kind=kLoop, calls=%fused_computation.16.clone.1 | loop fusion | flops 3670016 | bytes 2101248 | tf_op jit(solution)/shard_map/while/body/eval_jaxpr/cos | solution.py:17
  60.2 0.3 fusion.71
  60.5 0.3 convolution_add_fusion.2
  60.8 0.7 dynamic_slice.34
  62.2 4.1 %fusion.70 = (f32[512,512]{1,0:T(8,128)S(1)}, f32[512,512]{1,0:T(8,128)S(1)}) fusion(s32[512]{0:T(512)S(1)} %get-tuple-element.138, s32[512]{0:T(512)S(1)} %get-tuple-element.139), kind=kLoop, calls=%fused_computation.16.clone.1 | loop fusion | flops 3670016 | bytes 2101248 | tf_op jit(solution)/shard_map/while/body/eval_jaxpr/cos | solution.py:17
  66.4 0.3 fusion.71
  66.6 0.3 convolution_add_fusion.2
  66.9 0.0 copy-done
  66.9 0.4 add_reduce_fusion
  67.4 0.6 compare_select_fusion
  68.0 0.1 fusion.59
  68.1 31.6 %all_gather.3 = bf16[8,32,2,512]{3,1,0,2:T(8,128)(2,1)S(1)} all-gather(bf16[1,32,2,512]{3,1,0,2:T(8,128)(2,1)S(1)} %pad_maximum_fusion.1), channel_id=1, replica_groups=mesh['pair'=8,'row'=4] {'pair'}, dimensions={0}, use_global_device_ids=true | all-gather | bytes 589824 | tf_op jit(solution)/shard_map/all_gather | solution.py:91
  99.7 0.2 fusion.18
  99.9 2.3 %fusion.28 = f32[2,8,32,256]{3,2,1,0:T(8,128)S(1)} fusion(bf16[1,8,32,512]{3,2,1,0:T(8,128)(2,1)S(1)} %get-tuple-element.99, bf16[1,8,32,512]{3,2,1,0:T(8,128)(2,1)S(1)} %get-tuple-element.98, s32[256]{0:T(256)S(1)} %iota_add_fusion.3, s32[512]{0:T(512)S(1)} %iota_add_fusion.2, f32[512]{0:T(512)S(1)} %multiply_multiply_fusion), kind=kOutput, calls=%fused_computation.45 | convolution fusion | flops 136577024 | bytes 1053696 | tf_op jit(solution)/shard_map/dot_general | solution.py:38
  102.2 0.1 fusion.34
  102.3 0.1 multiply_reduce_fusion.1
  102.4 0.1 multiply_add_fusion.1
  102.5 0.1 multiply_subtract_fusion
  102.6 35.2 %all-reduce = (f32[32,8,8]{0,1,2:T(8,128)S(1)}, f32[32,8]{0,1:T(8,128)S(1)}) all-reduce(f32[32,8,8]{0,1,2:T(8,128)S(1)} %multiply_subtract_fusion, f32[32,8]{0,1:T(8,128)S(1)} %get-tuple-element.104), channel_id=1, replica_groups=mesh['pair'=8,'row'=4] {'pair'}, use_global_device_ids=true, to_apply=%region_5.6 | all-reduce | flops 2304 | bytes 18432 | tf_op jit(solution)/shard_map/psum | solution.py:105
  137.8 0.6 gather_fusion
  138.4 0.7 reduce_sum.57
  139.7 6.3 %psum.22 = f32[]{:T(128)} all-reduce(f32[]{:T(128)} %reduce_sum.57), channel_id=1, replica_groups=mesh['pair'=8,'row'=4] {'row'}, use_global_device_ids=true, to_apply=%region_7.8 | all-reduce | flops 1 | bytes 8 | tf_op jit(solution)/shard_map/psum | solution.py:107
  146.7 0.1 multiply_add_fusion
  146.8 0.1 copy.41
  146.9 23.5 %custom-call.11 = f32[32,8,8]{2,1,0:T(8,128)S(1)} custom-call(f32[32,8,8]{2,1,0:T(8,128)S(1)} %broadcast_multiply_fusion), custom_call_target="Cholesky" | custom-call | tf_op jit(solution)/shard_map/jit(cholesky)/cholesky | solution.py:111
  170.4 0.1 copy.42
  170.5 0.1 select_reduce_fusion
  170.6 0.1 select_bitcast_fusion
  170.7 0.7 custom-call.12
  171.5 0.5 dynamic-slice_bitcast_fusion
  (29 shorter events, 0.2 us)
Async XLA Ops:
  0.0 9.2 %copy-start.1 = (s32[8]{0:T(128)S(1)}, s32[8]{0:T(128)}, u32[]{:S(2)}) copy-start(s32[8]{0:T(128)} %param.8) | copy-start | bytes 100
  1.7 16.2 %all-to-all-start = ((bf16[32,512,8]{1,0,2:T(8,128)(2,1)}), bf16[32,512,8]{1,0,2:T(8,128)(2,1)S(1)}, u32[]{:S(2)}, u32[]{:S(2)}) async-start(bf16[32,512,8]{1,0,2:T(8,128)(2,1)} %copy.35), calls=%async_computation | async-start | bytes 524288 | tf_op jit(solution)/shard_map/all_to_all | solution.py:48
  18.0 49.0 %copy-start = (f32[1,32]{1,0:T(1,128)S(1)}, f32[1,32]{1,0:T(1,128)}, u32[]{:S(2)}) copy-start(f32[1,32]{1,0:T(1,128)} %param.7) | copy-start | bytes 388
where the time goes:
time: 172 us
  blocking collectives  73.1 us (42%)
  other arithmetic  60.2 us (35%)
  local copies, waits for them, and re-layouts  9.21 us (5%)
  waiting for transfers between devices  8.06 us (5%)
  starting transfers between devices  7.28 us (4%)
  matrix products  6.83 us (4%)
  loops' own time  5.79 us (3%)
    psum x1, blocking collectives, per_device(): hessian, gradient = lax.psum((hessian, gradient), 'pair')  35.2 us
    cos x8, other arithmetic, band_table(): return jnp.concatenate([jnp.cos(angles), jnp.sin(angles)], axis=1)  33.2 us
    all_gather x1, blocking collectives, per_device(): segment = lax.all_gather(own_spec[None], 'pair', axis=0, tiled=True)  31.6 us
    another operation x4, other arithmetic, per_device(): factor = jnp.linalg.cholesky(system)  23.6 us
    all_to_all x1, waiting for transfers between devices, per_device(): lax.all_to_all(records, 'pair', split_axis=2, concat_axis=1, tiled=True)  8.06 us
    all_to_all x1, starting transfers between devices, per_device(): lax.all_to_all(records, 'pair', split_axis=2, concat_axis=1, tiled=True)  7.28 us
    psum x1, blocking collectives, per_device(): trace_sum = lax.psum(jnp.sum(diagonal), 'row')  6.25 us
    another operation x1, loops' own time, per_device(): lax.scan(accumulate, jnp.zeros((channels, 2 * NF), jnp.float32), jnp.aran...  5.79 us
  transfers between devices with their start and end apart: 1, of which 1 were waited for; matrix products, arithmetic and copies ran while one was open for 0% of the time, Pallas kernels for 0%

commit v1 on v0

--- a/solution.py
+++ b/solution.py
@@ -45,7 +45,16 @@
     nblock = lax.axis_size("pair")
     block_rank = lax.axis_index("pair")
     quarter = lax.axis_index("row")
-    relaid = lax.all_to_all(records, "pair", split_axis=2, concat_axis=1, tiled=True)
+    shelves_create = lambda local_x, group_axis: jnp.concatenate(
+        lax.all_to_all(
+            jnp.stack(jnp.split(local_x, lax.axis_size(group_axis), axis=2), axis=0),
+            axis_name=group_axis,
+            split_axis=0,
+            concat_axis=0,
+        ),
+        axis=1,
+    )
+    relaid = shelves_create(records, "pair")
     signal = relaid[:, :, 0]
     channels = signal.shape[0]
     samples = signal.shape[1]

time: 172 us -> 178 us (1.035)
  local copies, waits for them, and re-layouts: 9.21 us -> 15.1 us
    split x0 -> x1, local copies, waits for them, and re-layouts: none -> 2.73 us  [per_device(): jnp.split(local_x, lax.axis_size(group_axis), axis=2)]
    unnamed x6 -> x12, local copies, waits for them, and re-layouts: 1.77 us -> 4.29 us
where the time goes in v1:
time: 178 us
  blocking collectives  73 us (41%)
  other arithmetic  60.2 us (34%)
  local copies, waits for them, and re-layouts  15.1 us (8%)
  waiting for transfers between devices  8.06 us (5%)
  starting transfers between devices  7.28 us (4%)
  matrix products  6.85 us (4%)
  loops' own time  5.76 us (3%)
    psum x1, blocking collectives, per_device(): hessian, gradient = lax.psum((hessian, gradient), 'pair')  35.2 us
    cos x8, other arithmetic, band_table(): return jnp.concatenate([jnp.cos(angles), jnp.sin(angles)], axis=1)  33.2 us
    all_gather x1, blocking collectives, per_device(): segment = lax.all_gather(own_spec[None], 'pair', axis=0, tiled=True)  31.6 us
    another operation x4, other arithmetic, per_device(): factor = jnp.linalg.cholesky(system)  23.6 us
    all_to_all x1, waiting for transfers between devices, per_device(): lax.all_to_all(jnp.stack(jnp.split(local_x, lax.axis_size(group_axis), ax...  8.06 us
    all_to_all x1, starting transfers between devices, per_device(): lax.all_to_all(jnp.stack(jnp.split(local_x, lax.axis_size(group_axis), ax...  7.28 us
    psum x1, blocking collectives, per_device(): trace_sum = lax.psum(jnp.sum(diagonal), 'row')  6.25 us
    another operation x1, loops' own time, per_device(): lax.scan(accumulate, jnp.zeros((channels, 2 * NF), jnp.float32), jnp.aran...  5.76 us
  transfers between devices with their start and end apart: 1, of which 1 were waited for; matrix products, arithmetic and copies ran while one was open for 0% of the time, Pallas kernels for 0%

profile of v1, /device:TPU:0, one launch (start us, length us, event | category | flops | bytes accessed | tf_op | source)
XLA Modules:
  0.0 177.8 jit_solution(12998180513503064285)
XLA Ops:
  0.0 2.7 %fusion.70 = (bf16[32,512,1]{1,2,0:T(2,128)(2,1)S(1)}, bf16[32,512,1]{1,2,0:T(2,128)(2,1)S(1)}, bf16[32,512,1]{1,2,0:T(2,128)(2,1)S(1)}, bf16[32,512,1]{1,2,0:T(...) fusion(bf16[32,512,8]{1,2,0:T(8,128)(2,1)} %param.6), kind=kLoop, calls=%fused_computation.128 | loop fusion | bytes 524288 | tf_op jit(solution)/shard_map/split | solution.py:50
  2.7 0.6 fusion.55
  3.4 0.6 fusion.54
  4.0 0.6 fusion.53
  4.6 0.6 fusion.52
  5.2 0.6 fusion.51
  5.8 0.6 fusion.50
  6.4 0.6 fusion.49
  7.0 0.6 fusion.48
  7.6 7.3 %all-to-all-start = ((bf16[8,32,512,1]{2,1,3,0:T(8,128)(2,1)}), bf16[8,32,512,1]{2,1,3,0:T(8,128)(2,1)S(1)}, u32[]{:S(2)}, u32[]{:S(2)}) async-start(bf16[8,32,512,1]{2,1,3,0:T(8,128)(2,1)} %fusion.48), calls=%async_computation | async-start | bytes 524288 | tf_op jit(solution)/shard_map/all_to_all | solution.py:49
  15.0 0.6 dynamic_slice.20
  15.8 8.1 %all-to-all-done = bf16[8,32,512,1]{2,1,3,0:T(8,128)(2,1)S(1)} async-done(((bf16[8,32,512,1]{2,1,3,0:T(8,128)(2,1)}), bf16[8,32,512,1]{2,1,3,0:T(8,128)(2,1)S(1)}, u32[]{:S(2)}, u32[]{:S(2)}) %all-to-all-start) | async-done | bytes 262176 | tf_op jit(solution)/shard_map/all_to_all | solution.py:49
  23.9 48.9 %while.13 = (s32[]{:T(128)}, f32[32,1024]{1,0:T(8,128)S(1)}, s32[8]{0:T(128)S(1)}, bf16[32,4096]{1,0:T(8,128)(2,1)S(1)}, s32[]{:T(128)}, /*index=5*/s32[1]{0:T(128)}, s32[]{:T(128)}, s32[]{:T(128)}) while((s32[]{:T(128)}, f32[32,1024]{1,0:T(8,128)S(1)}, s32[8]{0:T(128)S(1)}, bf16[32,4096]{1,0:T(8,128)(2,1)S(1)}, s32[]{:T(128)}, ...), condition=%wide.region_1.2_spmd.clone, body=%wide.region_0.1_spmd.clone.sunk | while | flops 75596808 | bytes 6889637 | solution.py:78
  23.9 0.7 dynamic_slice.34
  25.3 4.1 %fusion.79 = (f32[512,512]{1,0:T(8,128)S(1)}, f32[512,512]{1,0:T(8,128)S(1)}) fusion(s32[512]{0:T(512)S(1)} %get-tuple-element.146, s32[512]{0:T(512)S(1)} %get-tuple-element.147), kind=kLoop, calls=%fused_computation.16.clone.1 | loop fusion | flops 3670016 | bytes 2101248 | tf_op jit(solution)/shard_map/while/body/eval_jaxpr/cos | solution.py:17
  29.4 0.3 fusion.80
  29.7 0.3 convolution_add_fusion.2
  30.0 0.7 dynamic_slice.34
  31.4 4.1 %fusion.79 = (f32[512,512]{1,0:T(8,128)S(1)}, f32[512,512]{1,0:T(8,128)S(1)}) fusion(s32[512]{0:T(512)S(1)} %get-tuple-element.146, s32[512]{0:T(512)S(1)} %get-tuple-element.147), kind=kLoop, calls=%fused_computation.16.clone.1 | loop fusion | flops 3670016 | bytes 2101248 | tf_op jit(solution)/shard_map/while/body/eval_jaxpr/cos | solution.py:17
  35.5 0.3 fusion.80
  35.8 0.3 convolution_add_fusion.2
  36.1 0.7 dynamic_slice.34
  37.5 4.1 %fusion.79 = (f32[512,512]{1,0:T(8,128)S(1)}, f32[512,512]{1,0:T(8,128)S(1)}) fusion(s32[512]{0:T(512)S(1)} %get-tuple-element.146, s32[512]{0:T(512)S(1)} %get-tuple-element.147), kind=kLoop, calls=%fused_computation.16.clone.1 | loop fusion | flops 3670016 | bytes 2101248 | tf_op jit(solution)/shard_map/while/body/eval_jaxpr/cos | solution.py:17
  41.6 0.3 fusion.80
  41.9 0.3 convolution_add_fusion.2
  42.2 0.7 dynamic_slice.34
  43.6 4.1 %fusion.79 = (f32[512,512]{1,0:T(8,128)S(1)}, f32[512,512]{1,0:T(8,128)S(1)}) fusion(s32[512]{0:T(512)S(1)} %get-tuple-element.146, s32[512]{0:T(512)S(1)} %get-tuple-element.147), kind=kLoop, calls=%fused_computation.16.clone.1 | loop fusion | flops 3670016 | bytes 2101248 | tf_op jit(solution)/shard_map/while/body/eval_jaxpr/cos | solution.py:17
  47.8 0.3 fusion.80
  48.1 0.3 convolution_add_fusion.2
  48.3 0.7 dynamic_slice.34
  49.7 4.1 %fusion.79 = (f32[512,512]{1,0:T(8,128)S(1)}, f32[512,512]{1,0:T(8,128)S(1)}) fusion(s32[512]{0:T(512)S(1)} %get-tuple-element.146, s32[512]{0:T(512)S(1)} %get-tuple-element.147), kind=kLoop, calls=%fused_computation.16.clone.1 | loop fusion | flops 3670016 | bytes 2101248 | tf_op jit(solution)/shard_map/while/body/eval_jaxpr/cos | solution.py:17
  53.9 0.3 fusion.80
  54.2 0.3 convolution_add_fusion.2
  54.4 0.7 dynamic_slice.34
  55.8 4.1 %fusion.79 = (f32[512,512]{1,0:T(8,128)S(1)}, f32[512,512]{1,0:T(8,128)S(1)}) fusion(s32[512]{0:T(512)S(1)} %get-tuple-element.146, s32[512]{0:T(512)S(1)} %get-tuple-element.147), kind=kLoop, calls=%fused_computation.16.clone.1 | loop fusion | flops 3670016 | bytes 2101248 | tf_op jit(solution)/shard_map/while/body/eval_jaxpr/cos | solution.py:17
  60.0 0.3 fusion.80
  60.3 0.3 convolution_add_fusion.2
  60.6 0.7 dynamic_slice.34
  61.9 4.1 %fusion.79 = (f32[512,512]{1,0:T(8,128)S(1)}, f32[512,512]{1,0:T(8,128)S(1)}) fusion(s32[512]{0:T(512)S(1)} %get-tuple-element.146, s32[512]{0:T(512)S(1)} %get-tuple-element.147), kind=kLoop, calls=%fused_computation.16.clone.1 | loop fusion | flops 3670016 | bytes 2101248 | tf_op jit(solution)/shard_map/while/body/eval_jaxpr/cos | solution.py:17
  66.1 0.3 fusion.80
  66.4 0.3 convolution_add_fusion.2
  66.7 0.7 dynamic_slice.34
  68.1 4.1 %fusion.79 = (f32[512,512]{1,0:T(8,128)S(1)}, f32[512,512]{1,0:T(8,128)S(1)}) fusion(s32[512]{0:T(512)S(1)} %get-tuple-element.146, s32[512]{0:T(512)S(1)} %get-tuple-element.147), kind=kLoop, calls=%fused_computation.16.clone.1 | loop fusion | flops 3670016 | bytes 2101248 | tf_op jit(solution)/shard_map/while/body/eval_jaxpr/cos | solution.py:17
  72.2 0.3 fusion.80
  72.5 0.3 convolution_add_fusion.2
  72.8 0.4 add_reduce_fusion
  73.2 0.6 compare_select_fusion
  73.9 0.1 fusion.67
  74.0 31.6 %all_gather.3 = bf16[8,32,2,512]{3,1,0,2:T(8,128)(2,1)S(1)} all-gather(bf16[1,32,2,512]{3,1,0,2:T(8,128)(2,1)S(1)} %pad_maximum_fusion.1), channel_id=1, replica_groups=mesh['pair'=8,'row'=4] {'pair'}, dimensions={0}, use_global_device_ids=true | all-gather | bytes 589824 | tf_op jit(solution)/shard_map/all_gather | solution.py:100
  105.5 0.2 fusion.18
  105.7 2.3 %fusion.28 = f32[2,8,32,256]{3,2,1,0:T(8,128)S(1)} fusion(bf16[1,8,32,512]{3,2,1,0:T(8,128)(2,1)S(1)} %get-tuple-element.99, bf16[1,8,32,512]{3,2,1,0:T(8,128)(2,1)S(1)} %get-tuple-element.98, s32[256]{0:T(256)S(1)} %iota_add_fusion.3, s32[512]{0:T(512)S(1)} %iota_add_fusion.2, f32[512]{0:T(512)S(1)} %multiply_multiply_fusion), kind=kOutput, calls=%fused_computation.45 | convolution fusion | flops 136577024 | bytes 1053696 | tf_op jit(solution)/shard_map/dot_general | solution.py:38
  108.0 0.1 fusion.34
  108.2 0.1 multiply_reduce_fusion.1
  108.3 0.1 multiply_subtract_fusion
  108.4 35.2 %all-reduce = (f32[32,8,8]{0,1,2:T(8,128)S(1)}, f32[32,8]{0,1:T(8,128)S(1)}) all-reduce(f32[32,8,8]{0,1,2:T(8,128)S(1)} %multiply_subtract_fusion, f32[32,8]{0,1:T(8,128)S(1)} %get-tuple-element.112), channel_id=1, replica_groups=mesh['pair'=8,'row'=4] {'pair'}, use_global_device_ids=true, to_apply=%region_5.6 | all-reduce | flops 2304 | bytes 18432 | tf_op jit(solution)/shard_map/psum | solution.py:114
  143.7 0.6 gather_fusion
  144.2 0.7 reduce_sum.57
  145.6 6.3 %psum.22 = f32[]{:T(128)} all-reduce(f32[]{:T(128)} %reduce_sum.57), channel_id=1, replica_groups=mesh['pair'=8,'row'=4] {'row'}, use_global_device_ids=true, to_apply=%region_7.8 | all-reduce | flops 1 | bytes 8 | tf_op jit(solution)/shard_map/psum | solution.py:116
  152.6 0.1 copy.83
  152.8 23.5 %custom-call.11 = f32[32,8,8]{2,1,0:T(8,128)S(1)} custom-call(f32[32,8,8]{2,1,0:T(8,128)S(1)} %broadcast_multiply_fusion), custom_call_target="Cholesky" | custom-call | tf_op jit(solution)/shard_map/jit(cholesky)/cholesky | solution.py:120
  176.2 0.1 copy.84
  176.4 0.1 select_reduce_fusion
  176.6 0.7 custom-call.12
  177.3 0.5 dynamic-slice_bitcast_fusion
  (37 shorter events, 0.6 us)
Async XLA Ops:
  0.0 15.0 %copy-start.1 = (s32[8]{0:T(128)S(1)}, s32[8]{0:T(128)}, u32[]{:S(2)}) copy-start(s32[8]{0:T(128)} %param.8) | copy-start | bytes 100
  7.6 16.2 %all-to-all-start = ((bf16[8,32,512,1]{2,1,3,0:T(8,128)(2,1)}), bf16[8,32,512,1]{2,1,3,0:T(8,128)(2,1)S(1)}, u32[]{:S(2)}, u32[]{:S(2)}) async-start(bf16[8,32,512,1]{2,1,3,0:T(8,128)(2,1)} %fusion.48), calls=%async_computation | async-start | bytes 524288 | tf_op jit(solution)/shard_map/all_to_all | solution.py:49
  23.9 48.9 %copy-start = (f32[1,32]{1,0:T(1,128)S(1)}, f32[1,32]{1,0:T(1,128)}, u32[]{:S(2)}) copy-start(f32[1,32]{1,0:T(1,128)} %param.7) | copy-start | bytes 388
